TPU v7x, 128 devices: a whole 4x4x4 slice. The times are simulated.
128 devices in a mesh: cols: 32 (over y, z, core), grp: 4 (over x).
Axes of the slice: x: 4, y: 4, z: 4, core: 2. Of those that a mesh axis runs over, the one named last changes fastest.
Arguments:
- pilot_seed: int32 [16384], P(('cols', 'grp')), may hold values from 0 to 16777215
- delay_shift: int32 [131072], P(('cols', 'grp')), may hold values from 0 to 511
- active_column: int32 [512], replicated, may hold values from 0 to 131071
- channel: bfloat16 [512, 524288], P(None, ('cols', 'grp')), may hold values from -24 to 24
- initial_power: float32 [131072], P(('cols', 'grp')), may hold values from 0.0001 to 4, as said below
- noise_power: float32 [1], replicated, may hold values from 0.5 to 1.5
Outputs:
- powers: float32 [131072], P(('cols', 'grp'))
- gradient: float32 [131072], P(('cols', 'grp'))
Inputs may be any that keep to these rules, and one draw needn't show every extreme that they name: `initial_power`: every entry is positive.
All inputs are finite; a program needn't handle non-finite values.
Results may differ from a plain program's by a relative error of at most 0.0003.
Values sent between devices are 32-bit elements; how exact they have to be, the bound alone decides.
No kernel may reach another device: no remote copies, remote signals or barrier semaphores. Data moves between devices by JAX's collectives and lax.ppermute only.
A program may use at most 64 MiB of HBM per device.

v0:
```python
import math
import jax
import jax.numpy as jnp
from jax import lax
from jax.sharding import PartitionSpec as P

L = 512
DELAYS = 8
ITERS = 2
mult_first = 747796405
mult_second = 289133645
add_first = 1442695041
mult_third = 2073658381
contract_cols = (((1,), (1,)), ((), ()))


def pilot_matrix(seed_list, shifts):
    row_index = jnp.arange(L, dtype=jnp.int32)[:, None]
    offsets = (row_index - shifts[None, :] + L) % L
    hashed = (
        seed_list[None, :] * jnp.int32(mult_first)
        + offsets * jnp.int32(mult_second)
        + jnp.int32(add_first)
    )
    hashed = jnp.bitwise_xor(
        hashed, jnp.bitwise_and(jnp.right_shift(hashed, 15), jnp.int32(131071))
    )
    hashed = hashed * jnp.int32(mult_third)
    hashed = jnp.bitwise_xor(
        hashed, jnp.bitwise_and(jnp.right_shift(hashed, 13), jnp.int32(524287))
    )
    low_bit = jnp.bitwise_and(jnp.right_shift(hashed, 11), jnp.int32(1))
    return (1 - 2 * low_bit).astype(jnp.float32)


def exact_dot(left, right):
    return jnp.dot(left, right, precision=lax.Precision.HIGHEST, preferred_element_type=jnp.float32)


def shards(pilot_seed, delay_shift, active_column, channel, initial_power, noise_power):
    inv_root = 1.0 / math.sqrt(L)
    device_count = lax.axis_size("cols") * lax.axis_size("grp")
    total_samples = channel.shape[1] * device_count
    col_count = delay_shift.shape[0]
    dictionary = pilot_matrix(jnp.repeat(pilot_seed, DELAYS), delay_shift)
    first_col = lax.axis_index(("cols", "grp")) * col_count
    local_col = active_column - first_col
    owned = jnp.logical_and(local_col >= 0, local_col < col_count)
    clipped = jnp.clip(local_col, 0, col_count - 1)
    seeds_here = jnp.where(owned, pilot_seed[clipped // DELAYS], 0)
    shifts_here = jnp.where(owned, delay_shift[clipped], 0)
    seeds_all, shifts_all = lax.psum((seeds_here, shifts_here), ("cols", "grp"))
    active = pilot_matrix(seeds_all, shifts_all).astype(jnp.bfloat16)
    samples = (jnp.dot(active, channel, preferred_element_type=jnp.float32) * inv_root).astype(
        jnp.bfloat16
    )
    cov_part = lax.dot_general(samples, samples, contract_cols, preferred_element_type=jnp.float32)
    identity = jnp.eye(L, dtype=jnp.float32)
    noise_level = noise_power[0]

    def weighted(powers):
        return dictionary * (powers / L)[None, :]

    def model_part(powers):
        return lax.dot_general(
            weighted(powers),
            dictionary,
            contract_cols,
            precision=lax.Precision.HIGHEST,
            preferred_element_type=jnp.float32,
        )

    cov_sum, first_model = lax.psum((cov_part, model_part(initial_power)), ("cols", "grp"))
    sample_cov = cov_sum / total_samples + noise_level * identity
    powers = initial_power
    gradient = jnp.zeros_like(initial_power)
    summed = first_model
    for iteration in range(ITERS):
        if iteration > 0:
            model_summed = lax.psum(model_part(powers), ("cols", "grp"))
            summed = model_summed
        model_cov = summed + noise_level * identity
        factor = jnp.linalg.cholesky(model_cov)
        invert_result = jax.scipy.linalg.cho_solve((factor, True), identity)
        mapped = exact_dot(invert_result, dictionary)
        weighed = exact_dot(sample_cov, mapped)
        result = (jnp.sum(dictionary * mapped, axis=0) - jnp.sum(mapped * weighed, axis=0)) / L
        gradient = result
        powers = jnp.maximum(powers - gradient, 0.0)
    return (powers, gradient)


def solution(mesh):
    placed = (
        P(("cols", "grp")),
        P(("cols", "grp")),
        P(),
        P(None, ("cols", "grp")),
        P(("cols", "grp")),
        P(),
    )
    return jax.shard_map(
        shards,
        mesh=mesh,
        in_specs=placed,
        out_specs=(P(("cols", "grp")), P(("cols", "grp"))),
        check_vma=False,
    )
```

profile of v0, /device:TPU:1, one launch (start us, length us, event | category | flops | bytes accessed | tf_op | source)
XLA Modules:
  0.0 734.1 jit_solution(4290212688632799999)
XLA Ops:
  14.4 68.8 %all-reduce.1 = (s32[512]{0:T(512)S(1)}, s32[512]{0:T(512)S(1)}) all-reduce(s32[512]{0:T(512)S(1)} %broadcast_select_fusion, s32[512]{0:T(512)S(1)} %get-tuple-element.42), channel_id=1, replica_groups=mesh['cols'=32,'grp'=4] {'cols','grp'}, use_global_device_ids=true, to_apply=%region_11.14 | all-reduce | flops 1024 | bytes 8192 | tf_op jit(solution)/shard_map/psum | solution.py:52
  83.5 8.0 %fusion.2 = f32[512,512]{0,1:T(8,128)} fusion(f32[1024]{0:T(1024)S(1)} %broadcast_multiply_fusion.1, s32[1024]{0:T(1024)S(1)} %copy-done, s32[1024]{0:T(1024)S(1)} %mul.110), kind=kOutput, calls=%fused_computation.9 | convolution fusion | flops 3251109888 | bytes 1060864 | tf_op jit(solution)/shard_map/dot_general | solution.py:65
  91.5 13.1 %fusion.73 = f32[512,512]{0,1:T(8,128)} fusion(bf16[512,4096]{1,0:T(8,128)(2,1)} %param.12, s32[512]{0:T(512)S(1)} %get-tuple-element.36, s32[512]{0:T(512)S(1)} %broadcast_multiply_fusion.2), kind=kOutput, calls=%fused_computation.123 | convolution fusion | flops 4306763776 | bytes 5246976 | tf_op jit(solution)/shard_map/dot_general | solution.py:57
  105.4 146.8 %all-reduce.8.cloned.1.call-done = (f32[512,512]{0,1:T(8,128)}, f32[512,512]{0,1:T(8,128)}) async-done(((f32[512,512]{0,1:T(8,128)}, f32[512,512]{0,1:T(8,128)}), (f32[512,512]{0,1:T(8,128)}, f32[512,512]{0,1:T(8,128)})) %all-reduce.8.cloned.1.call-update) | async-done | bytes 2097168 | tf_op jit(solution)/shard_map/psum | solution.py:73
  257.5 11.7 %cholesky.286 = f32[128,128]{1,0:T(8,128)S(1)} custom-call(f32[128,128]{1,0:T(8,128)S(1)} %cholesky.426), custom_call_target="Cholesky" | custom-call | tf_op jit(solution)/shard_map/jit(cholesky)/cholesky | solution.py:83
  269.2 9.8 %custom-call.29 = f32[1,128,128]{1,2,0:T(8,128)S(1)} custom-call(f32[1,128,128]{2,1,0:T(8,128)S(1)} %get-tuple-element.67), custom_call_target="InvertDiagBlocksLowerTriangular" | custom-call | tf_op jit(solution)/shard_map/jit(cholesky)/cholesky | solution.py:83
  281.7 11.7 %cholesky.305 = f32[128,128]{1,0:T(8,128)S(1)} custom-call(f32[128,128]{1,0:T(8,128)S(1)} %cholesky.430), custom_call_target="Cholesky" | custom-call | tf_op jit(solution)/shard_map/jit(cholesky)/cholesky | solution.py:83
  293.4 10.0 %custom-call.30 = f32[1,128,128]{1,2,0:T(8,128)S(1)} custom-call(f32[1,128,128]{2,1,0:T(8,128)S(1)} %get-tuple-element.64), custom_call_target="InvertDiagBlocksLowerTriangular" | custom-call | tf_op jit(solution)/shard_map/jit(cholesky)/cholesky | solution.py:83
  305.0 11.7 %cholesky.326 = f32[128,128]{1,0:T(8,128)S(1)} custom-call(f32[128,128]{1,0:T(8,128)S(1)} %cholesky.435), custom_call_target="Cholesky" | custom-call | tf_op jit(solution)/shard_map/jit(cholesky)/cholesky | solution.py:83
  317.4 9.8 %custom-call.31 = f32[1,128,128]{1,2,0:T(8,128)S(1)} custom-call(f32[1,128,128]{2,1,0:T(8,128)S(1)} %get-tuple-element.61), custom_call_target="InvertDiagBlocksLowerTriangular" | custom-call | tf_op jit(solution)/shard_map/jit(cholesky)/cholesky | solution.py:83
  328.6 11.7 %cholesky.343 = f32[128,128]{1,0:T(8,128)S(1)} custom-call(f32[128,128]{1,0:T(8,128)S(1)} %convolution_subtract_fusion.17), custom_call_target="Cholesky" | custom-call | tf_op jit(solution)/shard_map/jit(cholesky)/cholesky | solution.py:83
  344.8 8.1 %while.4 = (s32[]{:T(128)}, f32[512,512]{1,0:T(8,128)S(1)}, s32[4,2]{0,1:T(2,128)S(1)}, f32[4,128,128]{2,1,0:T(8,128)S(1)}, s32[]{:T(128)}) while((s32[]{:T(128)}, f32[512,512]{1,0:T(8,128)S(1)}, s32[4,2]{0,1:T(2,128)S(1)}, f32[4,128,128]{2,1,0:T(8,128)S(1)}, s32[]{:T(128)}) %tuple.60), condition=%wide.while_cond, body=%wide.while_body.sunk | while | flops 2 | bytes 131181 | solution.py:84
  353.0 39.3 %custom-call.32 = f32[4,128,128]{1,2,0:T(8,128)S(1)} custom-call(f32[4,128,128]{2,1,0:T(8,128)S(1)} %get-tuple-element.18), custom_call_target="InvertDiagBlocksLowerTriangular" | custom-call | tf_op jit(solution)/shard_map/jit(_cho_solve)/triangular_solve | solution.py:84
  411.2 8.0 %fusion = f32[512,512]{0,1:T(8,128)} fusion(f32[1024]{0:T(1024)S(1)} %broadcast_multiply_fusion, s32[1024]{0:T(1024)S(1)} %copy-done, s32[1024]{0:T(1024)S(1)} %mul.110), kind=kOutput, calls=%fused_computation.7 | convolution fusion | flops 3251109888 | bytes 1060864 | tf_op jit(solution)/shard_map/dot_general | solution.py:65
  419.2 146.9 %all-reduce.6.cloned.1.call-done = f32[512,512]{0,1:T(8,128)} async-done(((f32[512,512]{0,1:T(8,128)}), f32[512,512]{0,1:T(8,128)}) %all-reduce.6.cloned.1.call-update) | async-done | bytes 1048592 | tf_op jit(solution)/shard_map/psum | solution.py:80
  571.8 11.7 %cholesky.358 = f32[128,128]{1,0:T(8,128)S(1)} custom-call(f32[128,128]{1,0:T(8,128)S(1)} %cholesky.439), custom_call_target="Cholesky" | custom-call | tf_op jit(solution)/shard_map/jit(cholesky)/cholesky | solution.py:83
  583.7 9.8 %custom-call.33 = f32[1,128,128]{1,2,0:T(8,128)S(1)} custom-call(f32[1,128,128]{2,1,0:T(8,128)S(1)} %get-tuple-element.57), custom_call_target="InvertDiagBlocksLowerTriangular" | custom-call | tf_op jit(solution)/shard_map/jit(cholesky)/cholesky | solution.py:83
  596.0 11.7 %cholesky.377 = f32[128,128]{1,0:T(8,128)S(1)} custom-call(f32[128,128]{1,0:T(8,128)S(1)} %cholesky.443), custom_call_target="Cholesky" | custom-call | tf_op jit(solution)/shard_map/jit(cholesky)/cholesky | solution.py:83
  609.0 10.0 %custom-call.34 = f32[1,128,128]{1,2,0:T(8,128)S(1)} custom-call(f32[1,128,128]{2,1,0:T(8,128)S(1)} %get-tuple-element.54), custom_call_target="InvertDiagBlocksLowerTriangular" | custom-call | tf_op jit(solution)/shard_map/jit(cholesky)/cholesky | solution.py:83
  620.6 11.7 %cholesky.398 = f32[128,128]{1,0:T(8,128)S(1)} custom-call(f32[128,128]{1,0:T(8,128)S(1)} %cholesky.448), custom_call_target="Cholesky" | custom-call | tf_op jit(solution)/shard_map/jit(cholesky)/cholesky | solution.py:83
  633.0 9.8 %custom-call.35 = f32[1,128,128]{1,2,0:T(8,128)S(1)} custom-call(f32[1,128,128]{2,1,0:T(8,128)S(1)} %get-tuple-element.51), custom_call_target="InvertDiagBlocksLowerTriangular" | custom-call | tf_op jit(solution)/shard_map/jit(cholesky)/cholesky | solution.py:83
  644.3 11.7 %cholesky.415 = f32[128,128]{1,0:T(8,128)S(1)} custom-call(f32[128,128]{1,0:T(8,128)S(1)} %convolution_subtract_fusion.16), custom_call_target="Cholesky" | custom-call | tf_op jit(solution)/shard_map/jit(cholesky)/cholesky | solution.py:83
  659.5 8.5 %while.5 = (s32[]{:T(128)}, f32[512,512]{1,0:T(8,128)S(1)}, s32[4,2]{0,1:T(2,128)S(1)}, f32[4,128,128]{2,1,0:T(8,128)S(1)}, s32[]{:T(128)}) while((s32[]{:T(128)}, f32[512,512]{1,0:T(8,128)S(1)}, s32[4,2]{0,1:T(2,128)S(1)}, f32[4,128,128]{2,1,0:T(8,128)S(1)}, s32[]{:T(128)}) %tuple.71), condition=%wide.while_cond.clone, body=%wide.while_body.clone.sunk | while | flops 2 | bytes 131181 | solution.py:84
  667.9 39.5 %custom-call.36 = f32[4,128,128]{1,2,0:T(8,128)S(1)} custom-call(f32[4,128,128]{2,1,0:T(8,128)S(1)} %get-tuple-element.19), custom_call_target="InvertDiagBlocksLowerTriangular" | custom-call | tf_op jit(solution)/shard_map/jit(_cho_solve)/triangular_solve | solution.py:84
  (140 shorter events, 89.9 us)
Async XLA Ops:
  7.2 4.9 copy-start.6
  7.2 4.9 copy-start
  7.2 245.0 %all-reduce.8.cloned.1.call-start = ((), (), s32[]{:S(2)}) async-start(), calls=%async_computation.1 | async-start | bytes 4194304 | tf_op jit(solution)/shard_map/psum | solution.py:73
  8.6 74.8 %copy-start.5 = (f32[1024]{0:T(1024)S(1)}, f32[1024]{0:T(1024)}, u32[]{:S(2)}) copy-start(f32[1024]{0:T(1024)} %param.13) | copy-start | bytes 12292
  104.6 461.5 %all-reduce.6.cloned.1.call-start = ((), (), s32[]{:S(2)}) async-start(), calls=%async_computation | async-start | bytes 2097152 | tf_op jit(solution)/shard_map/psum | solution.py:80
  252.2 2.8 copy-start.1
  256.4 1.0 copy-start.4
  400.2 7.3 copy-start.7
  566.1 3.2 copy-start.2
  570.7 1.0 copy-start.3
  715.4 7.4 %copy-start.8 = (f32[512,512]{0,1:T(8,128)S(1)}, f32[512,512]{0,1:T(8,128)}, u32[]{:S(2)}) copy-start(f32[512,512]{0,1:T(8,128)} %get-tuple-element.39) | copy-start | bytes 3145732
Sparse Core Ops, SparseCore 0:
  104.7 147.4 all-reduce.7
  419.3 146.7 all-reduce.5
where the time goes:
time: 737 us; the launch traced here: 734 us
  waiting for transfers between devices  294 us (40%)
  other arithmetic  245 us (33%)
  matrix products  77.5 us (11%)
  blocking collectives  68.8 us (9%)
  local copies, waits for them, and re-layouts  27.8 us (4%)
  between operations  20.7 us (3%)
    another operation x29, other arithmetic, shards(): factor = jnp.linalg.cholesky(model_cov)  158 us
    psum x1, waiting for transfers between devices, shards(): model_summed = lax.psum(model_part(powers), ('cols', 'grp'))  147 us
    psum x1, waiting for transfers between devices, shards(): lax.psum((cov_part, model_part(initial_power)), ('cols', 'grp'))  147 us
    another operation x5, other arithmetic, shards(): invert_result = jax.scipy.linalg.cho_solve((factor, True), identity)  79.1 us
    psum x1, blocking collectives, shards(): seeds_all, shifts_all = lax.psum((seeds_here, shifts_here), ('cols', 'grp'))  68.8 us
    dot_general x4, matrix products, exact_dot(): jnp.dot(left, right, precision=lax.Precision.HIGHEST, preferred_element_t...  21.9 us
    another operation x27, local copies, waits for them, and re-layouts, shards(): invert_result = jax.scipy.linalg.cho_solve((factor, True), identity)  16.5 us
    dot_general x2, matrix products, model_part(): lax.dot_general(weighted(powers), dictionary, contract_cols, precision=la...  16 us
  transfers between devices with their start and end apart: 2, of which 2 were waited for; matrix products, arithmetic and copies ran while one was open for 0% of the time, Pallas kernels for 0%

commit v1 on v0

--- a/solution.py
+++ b/solution.py
@@ -49,7 +49,7 @@
     clipped = jnp.clip(local_col, 0, col_count - 1)
     seeds_here = jnp.where(owned, pilot_seed[clipped // DELAYS], 0)
     shifts_here = jnp.where(owned, delay_shift[clipped], 0)
-    seeds_all, shifts_all = lax.psum((seeds_here, shifts_here), ("cols", "grp"))
+    seeds_all, shifts_all = lax.psum(lax.psum((seeds_here, shifts_here), "cols"), "grp")
     active = pilot_matrix(seeds_all, shifts_all).astype(jnp.bfloat16)
     samples = (jnp.dot(active, channel, preferred_element_type=jnp.float32) * inv_root).astype(
         jnp.bfloat16

time: 737 us -> 702 us (0.953); the launches traced: 734 us -> 691 us
  blocking collectives: 68.8 us -> 22.9 us
    psum x1 -> x2, blocking collectives: 68.8 us -> 22.9 us  [the longest x1 15.7 us: shards(): lax.psum((seeds_here, shifts_here), 'cols')]
where the time goes in v1:
time: 702 us; the launch traced here: 691 us
  waiting for transfers between devices  297 us (42%)
  other arithmetic  245 us (35%)
  matrix products  77.4 us (11%)
  local copies, waits for them, and re-layouts  27.8 us (4%)
  blocking collectives  22.9 us (3%)
  between operations  20.9 us (3%)
    another operation x29, other arithmetic, shards(): factor = jnp.linalg.cholesky(model_cov)  158 us
    psum x1, waiting for transfers between devices, shards(): lax.psum((cov_part, model_part(initial_power)), ('cols', 'grp'))  150 us
    psum x1, waiting for transfers between devices, shards(): model_summed = lax.psum(model_part(powers), ('cols', 'grp'))  147 us
    another operation x5, other arithmetic, shards(): invert_result = jax.scipy.linalg.cho_solve((factor, True), identity)  79.1 us
    dot_general x4, matrix products, exact_dot(): jnp.dot(left, right, precision=lax.Precision.HIGHEST, preferred_element_t...  21.8 us
    another operation x27, local copies, waits for them, and re-layouts, shards(): invert_result = jax.scipy.linalg.cho_solve((factor, True), identity)  16.5 us
    dot_general x2, matrix products, model_part(): lax.dot_general(weighted(powers), dictionary, contract_cols, precision=la...  16 us
    psum x1, blocking collectives, shards(): lax.psum((seeds_here, shifts_here), 'cols')  15.7 us
  transfers between devices with their start and end apart: 2, of which 2 were waited for; matrix products, arithmetic and copies ran while one was open for 0% of the time, Pallas kernels for 0%

profile of v1, /device:TPU:1, one launch (start us, length us, event | category | flops | bytes accessed | tf_op | source)
XLA Modules:
  0.0 691.4 jit_solution(5540285398355207402)
XLA Ops:
  14.4 15.7 %all-reduce.1 = (s32[512]{0:T(512)S(1)}, s32[512]{0:T(512)S(1)}) all-reduce(s32[512]{0:T(512)S(1)} %broadcast_select_fusion, s32[512]{0:T(512)S(1)} %get-tuple-element.44), channel_id=1, replica_groups=mesh['cols'=32,'grp'=4] {'cols'}, use_global_device_ids=true, to_apply=%region_12.15 | all-reduce | flops 1024 | bytes 8192 | tf_op jit(solution)/shard_map/psum | solution.py:52
  37.5 8.0 %fusion.2 = f32[512,512]{0,1:T(8,128)} fusion(f32[1024]{0:T(1024)S(1)} %broadcast_multiply_fusion.1, s32[1024]{0:T(1024)S(1)} %copy-done, s32[1024]{0:T(1024)S(1)} %mul.110), kind=kOutput, calls=%fused_computation.9 | convolution fusion | flops 3251109888 | bytes 1060864 | tf_op jit(solution)/shard_map/dot_general | solution.py:65
  45.5 13.0 %fusion.73 = f32[512,512]{0,1:T(8,128)} fusion(bf16[512,4096]{1,0:T(8,128)(2,1)} %param.12, s32[512]{0:T(512)S(1)} %get-tuple-element.38, s32[512]{0:T(512)S(1)} %broadcast_multiply_fusion.2), kind=kOutput, calls=%fused_computation.123 | convolution fusion | flops 4306763776 | bytes 5246976 | tf_op jit(solution)/shard_map/dot_general | solution.py:57
  59.4 150.0 %all-reduce.9.cloned.1.call-done = (f32[512,512]{0,1:T(8,128)}, f32[512,512]{0,1:T(8,128)}) async-done(((f32[512,512]{0,1:T(8,128)}, f32[512,512]{0,1:T(8,128)}), (f32[512,512]{0,1:T(8,128)}, f32[512,512]{0,1:T(8,128)})) %all-reduce.9.cloned.1.call-update) | async-done | bytes 2097168 | tf_op jit(solution)/shard_map/psum | solution.py:73
  214.6 11.7 %cholesky.286 = f32[128,128]{1,0:T(8,128)S(1)} custom-call(f32[128,128]{1,0:T(8,128)S(1)} %cholesky.426), custom_call_target="Cholesky" | custom-call | tf_op jit(solution)/shard_map/jit(cholesky)/cholesky | solution.py:83
  226.5 9.8 %custom-call.29 = f32[1,128,128]{1,2,0:T(8,128)S(1)} custom-call(f32[1,128,128]{2,1,0:T(8,128)S(1)} %get-tuple-element.69), custom_call_target="InvertDiagBlocksLowerTriangular" | custom-call | tf_op jit(solution)/shard_map/jit(cholesky)/cholesky | solution.py:83
  238.8 11.7 %cholesky.305 = f32[128,128]{1,0:T(8,128)S(1)} custom-call(f32[128,128]{1,0:T(8,128)S(1)} %cholesky.430), custom_call_target="Cholesky" | custom-call | tf_op jit(solution)/shard_map/jit(cholesky)/cholesky | solution.py:83
  250.6 10.0 %custom-call.30 = f32[1,128,128]{1,2,0:T(8,128)S(1)} custom-call(f32[1,128,128]{2,1,0:T(8,128)S(1)} %get-tuple-element.66), custom_call_target="InvertDiagBlocksLowerTriangular" | custom-call | tf_op jit(solution)/shard_map/jit(cholesky)/cholesky | solution.py:83
  262.1 11.7 %cholesky.326 = f32[128,128]{1,0:T(8,128)S(1)} custom-call(f32[128,128]{1,0:T(8,128)S(1)} %cholesky.435), custom_call_target="Cholesky" | custom-call | tf_op jit(solution)/shard_map/jit(cholesky)/cholesky | solution.py:83
  274.5 9.8 %custom-call.31 = f32[1,128,128]{1,2,0:T(8,128)S(1)} custom-call(f32[1,128,128]{2,1,0:T(8,128)S(1)} %get-tuple-element.63), custom_call_target="InvertDiagBlocksLowerTriangular" | custom-call | tf_op jit(solution)/shard_map/jit(cholesky)/cholesky | solution.py:83
  285.8 11.7 %cholesky.343 = f32[128,128]{1,0:T(8,128)S(1)} custom-call(f32[128,128]{1,0:T(8,128)S(1)} %convolution_subtract_fusion.17), custom_call_target="Cholesky" | custom-call | tf_op jit(solution)/shard_map/jit(cholesky)/cholesky | solution.py:83
  302.0 8.1 %while.4 = (s32[]{:T(128)}, f32[512,512]{1,0:T(8,128)S(1)}, s32[4,2]{0,1:T(2,128)S(1)}, f32[4,128,128]{2,1,0:T(8,128)S(1)}, s32[]{:T(128)}) while((s32[]{:T(128)}, f32[512,512]{1,0:T(8,128)S(1)}, s32[4,2]{0,1:T(2,128)S(1)}, f32[4,128,128]{2,1,0:T(8,128)S(1)}, s32[]{:T(128)}) %tuple.60), condition=%wide.while_cond, body=%wide.while_body.sunk | while | flops 2 | bytes 131181 | solution.py:84
  310.1 39.3 %custom-call.32 = f32[4,128,128]{1,2,0:T(8,128)S(1)} custom-call(f32[4,128,128]{2,1,0:T(8,128)S(1)} %get-tuple-element.18), custom_call_target="InvertDiagBlocksLowerTriangular" | custom-call | tf_op jit(solution)/shard_map/jit(_cho_solve)/triangular_solve | solution.py:84
  368.3 8.0 %fusion = f32[512,512]{0,1:T(8,128)} fusion(f32[1024]{0:T(1024)S(1)} %broadcast_multiply_fusion, s32[1024]{0:T(1024)S(1)} %copy-done, s32[1024]{0:T(1024)S(1)} %mul.110), kind=kOutput, calls=%fused_computation.7 | convolution fusion | flops 3251109888 | bytes 1060864 | tf_op jit(solution)/shard_map/dot_general | solution.py:65
  376.4 147.0 %all-reduce.7.cloned.1.call-done = f32[512,512]{0,1:T(8,128)} async-done(((f32[512,512]{0,1:T(8,128)}), f32[512,512]{0,1:T(8,128)}) %all-reduce.7.cloned.1.call-update) | async-done | bytes 1048592 | tf_op jit(solution)/shard_map/psum | solution.py:80
  529.0 11.7 %cholesky.358 = f32[128,128]{1,0:T(8,128)S(1)} custom-call(f32[128,128]{1,0:T(8,128)S(1)} %cholesky.439), custom_call_target="Cholesky" | custom-call | tf_op jit(solution)/shard_map/jit(cholesky)/cholesky | solution.py:83
  540.9 9.8 %custom-call.33 = f32[1,128,128]{1,2,0:T(8,128)S(1)} custom-call(f32[1,128,128]{2,1,0:T(8,128)S(1)} %get-tuple-element.59), custom_call_target="InvertDiagBlocksLowerTriangular" | custom-call | tf_op jit(solution)/shard_map/jit(cholesky)/cholesky | solution.py:83
  553.2 11.7 %cholesky.377 = f32[128,128]{1,0:T(8,128)S(1)} custom-call(f32[128,128]{1,0:T(8,128)S(1)} %cholesky.443), custom_call_target="Cholesky" | custom-call | tf_op jit(solution)/shard_map/jit(cholesky)/cholesky | solution.py:83
  566.3 10.0 %custom-call.34 = f32[1,128,128]{1,2,0:T(8,128)S(1)} custom-call(f32[1,128,128]{2,1,0:T(8,128)S(1)} %get-tuple-element.56), custom_call_target="InvertDiagBlocksLowerTriangular" | custom-call | tf_op jit(solution)/shard_map/jit(cholesky)/cholesky | solution.py:83
  577.8 11.7 %cholesky.398 = f32[128,128]{1,0:T(8,128)S(1)} custom-call(f32[128,128]{1,0:T(8,128)S(1)} %cholesky.448), custom_call_target="Cholesky" | custom-call | tf_op jit(solution)/shard_map/jit(cholesky)/cholesky | solution.py:83
  590.2 9.8 %custom-call.35 = f32[1,128,128]{1,2,0:T(8,128)S(1)} custom-call(f32[1,128,128]{2,1,0:T(8,128)S(1)} %get-tuple-element.53), custom_call_target="InvertDiagBlocksLowerTriangular" | custom-call | tf_op jit(solution)/shard_map/jit(cholesky)/cholesky | solution.py:83
  601.5 11.7 %cholesky.415 = f32[128,128]{1,0:T(8,128)S(1)} custom-call(f32[128,128]{1,0:T(8,128)S(1)} %convolution_subtract_fusion.16), custom_call_target="Cholesky" | custom-call | tf_op jit(solution)/shard_map/jit(cholesky)/cholesky | solution.py:83
  616.7 8.5 %while.5 = (s32[]{:T(128)}, f32[512,512]{1,0:T(8,128)S(1)}, s32[4,2]{0,1:T(2,128)S(1)}, f32[4,128,128]{2,1,0:T(8,128)S(1)}, s32[]{:T(128)}) while((s32[]{:T(128)}, f32[512,512]{1,0:T(8,128)S(1)}, s32[4,2]{0,1:T(2,128)S(1)}, f32[4,128,128]{2,1,0:T(8,128)S(1)}, s32[]{:T(128)}) %tuple.71), condition=%wide.while_cond.clone, body=%wide.while_body.clone.sunk | while | flops 2 | bytes 131181 | solution.py:84
  625.2 39.5 %custom-call.36 = f32[4,128,128]{1,2,0:T(8,128)S(1)} custom-call(f32[4,128,128]{2,1,0:T(8,128)S(1)} %get-tuple-element.19), custom_call_target="InvertDiagBlocksLowerTriangular" | custom-call | tf_op jit(solution)/shard_map/jit(_cho_solve)/triangular_solve | solution.py:84
  (141 shorter events, 97.0 us)
Async XLA Ops:
  7.2 4.9 copy-start.6
  7.2 4.9 copy-start
  7.2 202.1 %all-reduce.9.cloned.1.call-start = ((), (), s32[]{:S(2)}) async-start(), calls=%async_computation.1 | async-start | bytes 4194304 | tf_op jit(solution)/shard_map/psum | solution.py:73
  8.6 28.9 %copy-start.5 = (f32[1024]{0:T(1024)S(1)}, f32[1024]{0:T(1024)}, u32[]{:S(2)}) copy-start(f32[1024]{0:T(1024)} %param.13) | copy-start | bytes 12292
  58.5 464.8 %all-reduce.7.cloned.1.call-start = ((), (), s32[]{:S(2)}) async-start(), calls=%async_computation | async-start | bytes 2097152 | tf_op jit(solution)/shard_map/psum | solution.py:80
  209.3 2.8 copy-start.1
  213.6 1.0 copy-start.4
  357.3 7.3 %copy-start.7 = (f32[512,512]{0,1:T(8,128)S(1)}, f32[512,512]{0,1:T(8,128)}, u32[]{:S(2)}) copy-start(f32[512,512]{0,1:T(8,128)} %get-tuple-element.41) | copy-start | bytes 3145732
  523.3 3.2 copy-start.2
  528.0 1.0 copy-start.3
  672.6 7.4 %copy-start.8 = (f32[512,512]{0,1:T(8,128)S(1)}, f32[512,512]{0,1:T(8,128)}, u32[]{:S(2)}) copy-start(f32[512,512]{0,1:T(8,128)} %get-tuple-element.41) | copy-start | bytes 3145732
Sparse Core Ops, SparseCore 0:
  58.7 150.6 all-reduce.8
  376.5 146.7 all-reduce.6
